TPU v7x, 32 devices: a whole 2x2x4 slice. The times are simulated.
32 devices in a mesh: dp: 8 (over y, x, core), tensor: 4 (over z).
Axes of the slice: x: 2, y: 2, z: 4, core: 2. Of those that a mesh axis runs over, the one named last changes fastest.
Arguments:
- block_in: float32 [4096, 1024], P(('dp', 'tensor')), may hold values from -6 to 6
- cotangent: float32 [4096, 1024], P(('dp', 'tensor')), may hold values from -6 to 6
- routes: int32 [4096, 8], P('dp'), may hold values from 0 to 15, all different within a row; in each aligned block of 512 rows (0 to 511, 512 to 1023, ...) at most 288 rows name the same one
- gate_weights: float32 [4096, 8], P('dp'), may hold values from 0.02 to 0.3
- norm_gains: float32 [2, 1024], P(None, 'dp'), may hold values from 0.5 to 1.5
- attention_weight: float32 [4, 1024, 512], P(None, 'dp', 'tensor'), may hold values from -0.1875 to 0.1875
- output_weight: float32 [2, 1024, 512], P(None, 'dp', 'tensor'), may hold values from -0.75 to 0.75
- w_gate_up: float32 [16, 2, 1024, 512], P(None, None, 'dp', 'tensor'), may hold values from -0.1875 to 0.1875
- w_down: float32 [16, 1024, 512], P(None, 'dp', 'tensor'), may hold values from -0.75 to 0.75
- m_gains: float32 [2, 1024], P(None, 'dp'), may hold values from -128 to 128
- v_gains: float32 [2, 1024], P(None, 'dp'), may hold values from 100 to 10000
- attention_first_moment: float32 [4, 1024, 512], P(None, 'dp', 'tensor'), may hold values from -12 to 12
- attention_second_moment: float32 [4, 1024, 512], P(None, 'dp', 'tensor'), may hold values from 1 to 100
- output_first_moment: float32 [2, 1024, 512], P(None, 'dp', 'tensor'), may hold values from -16 to 16
- output_second_moment: float32 [2, 1024, 512], P(None, 'dp', 'tensor'), may hold values from 1 to 100
- m_gate_up: float32 [16, 2, 1024, 512], P(None, None, 'dp', 'tensor'), may hold values from -32 to 32
- v_gate_up: float32 [16, 2, 1024, 512], P(None, None, 'dp', 'tensor'), may hold values from 10 to 1000
- m_down: float32 [16, 1024, 512], P(None, 'dp', 'tensor'), may hold values from -12 to 12
- v_down: float32 [16, 1024, 512], P(None, 'dp', 'tensor'), may hold values from 1 to 100
Outputs:
- block_out: float32 [4096, 1024], P(('dp', 'tensor'))
- input_grad: float32 [4096, 1024], P(('dp', 'tensor'))
- grad_gains: float32 [2, 1024], P(None, 'dp')
- grad_attn: float32 [4, 1024, 512], P(None, 'dp', 'tensor')
- grad_out: float32 [2, 1024, 512], P(None, 'dp', 'tensor')
- grad_gate_up: float32 [16, 2, 1024, 512], P(None, None, 'dp', 'tensor')
- grad_down: float32 [16, 1024, 512], P(None, 'dp', 'tensor')
- new_gains: float32 [2, 1024], P(None, 'dp')
- new_attn: float32 [4, 1024, 512], P(None, 'dp', 'tensor')
- new_out: float32 [2, 1024, 512], P(None, 'dp', 'tensor')
- new_gate_up: float32 [16, 2, 1024, 512], P(None, None, 'dp', 'tensor')
- new_down: float32 [16, 1024, 512], P(None, 'dp', 'tensor')
- new_m_gains: float32 [2, 1024], P(None, 'dp')
- new_v_gains: float32 [2, 1024], P(None, 'dp')
- new_m_attn: float32 [4, 1024, 512], P(None, 'dp', 'tensor')
- new_v_attn: float32 [4, 1024, 512], P(None, 'dp', 'tensor')
- new_m_out: float32 [2, 1024, 512], P(None, 'dp', 'tensor')
- new_v_out: float32 [2, 1024, 512], P(None, 'dp', 'tensor')
- new_m_gate_up: float32 [16, 2, 1024, 512], P(None, None, 'dp', 'tensor')
- new_v_gate_up: float32 [16, 2, 1024, 512], P(None, None, 'dp', 'tensor')
- new_m_down: float32 [16, 1024, 512], P(None, 'dp', 'tensor')
- new_v_down: float32 [16, 1024, 512], P(None, 'dp', 'tensor')
Inputs may be any that keep to these rules, and one draw needn't show every extreme that they name: `routes`: each row names 8 different experts. Within each aligned block of 512 rows no expert is named by more than 288 rows, and in some block one expert is named by exactly 288 rows.
All inputs are finite; a program needn't handle non-finite values.
Results may differ from a plain program's by a relative error of at most 0.015.
The roundings to bfloat16 on the way count: a program that leaves them out, or rounds other values in their place, can miss the bound.
Values may be sent and summed in bfloat16 or wider, within the bound.
A program may use at most 192 MiB of HBM per device.

v0:
```python
import jax
import jax.numpy as jnp
from jax import lax
from jax.sharding import PartitionSpec as P

HEAD_SIZE = 64
SEQ = 512
STEP = 3
norm_eps = 1e-05
beta_one = 0.9
beta_two = 0.95
adam_eps = 1e-08
rate_matrix = 0.02
rate_gain = 0.2
decay_matrix = 0.1
rope_base = 10000.0


def rope_tables(length, width):
    half_width = width // 2
    frequency = rope_base ** (-(2.0 * jnp.arange(half_width, dtype=jnp.float32)) / width)
    angles = jnp.arange(length, dtype=jnp.float32)[:, None] * frequency[None, :]
    return (jnp.cos(angles)[:, None, :], jnp.sin(angles)[:, None, :])


def rotate(vectors, cos_table, sine_table):
    half_width = vectors.shape[-1] // 2
    lower_half = vectors[..., :half_width]
    upper_half = vectors[..., half_width:]
    return jnp.concatenate(
        [
            lower_half * cos_table - upper_half * sine_table,
            upper_half * cos_table + lower_half * sine_table,
        ],
        axis=-1,
    )


def unrotate(vectors, cos_table, sine_table):
    half_width = vectors.shape[-1] // 2
    lower_half = vectors[..., :half_width]
    upper_half = vectors[..., half_width:]
    return jnp.concatenate(
        [
            lower_half * cos_table + upper_half * sine_table,
            upper_half * cos_table - lower_half * sine_table,
        ],
        axis=-1,
    )


def causal_scores(queries, keys_rot):
    scale = queries.shape[-1] ** (-0.5)
    scores = (
        jnp.einsum("jqgh,kgh->jgqk", queries, keys_rot, preferred_element_type=jnp.float32) * scale
    )
    length = scores.shape[-1]
    allowed = lax.broadcasted_iota(jnp.int32, (length, length), 0) >= lax.broadcasted_iota(
        jnp.int32, (length, length), 1
    )
    return jnp.where(allowed, scores, -jnp.inf)


def attend(items):
    queries, keys_rot, values = items
    scores = causal_scores(queries, keys_rot)
    log_totals = jax.nn.logsumexp(scores, axis=-1)
    softmax_b = jnp.exp(scores - log_totals[..., None]).astype(jnp.bfloat16)
    attended = jnp.einsum(
        "jgqk,kgh->jqgh", softmax_b, values, preferred_element_type=jnp.float32
    ).astype(jnp.bfloat16)
    return (attended, log_totals)


def attend_back(items):
    queries, keys_rot, values, attended, log_totals, attended_cot = items
    scale = queries.shape[-1] ** (-0.5)
    scores = causal_scores(queries, keys_rot)
    softmax_f = jnp.exp(scores - log_totals[..., None])
    softmax_b = softmax_f.astype(jnp.bfloat16)
    value_cot = jnp.einsum(
        "jgqk,jqgh->kgh", softmax_b, attended_cot, preferred_element_type=jnp.float32
    )
    weight_cot = jnp.einsum(
        "jqgh,kgh->jgqk", attended_cot, values, preferred_element_type=jnp.float32
    )
    row_dots = jnp.einsum(
        "jqgh,jqgh->jgq", attended_cot, attended, preferred_element_type=jnp.float32
    )
    score_cot = (softmax_f * (weight_cot - row_dots[..., None])).astype(jnp.bfloat16)
    query_cot = (
        jnp.einsum("jgqk,kgh->jqgh", score_cot, keys_rot, preferred_element_type=jnp.float32)
        * scale
    )
    key_cot = (
        jnp.einsum("jgqk,jqgh->kgh", score_cot, queries, preferred_element_type=jnp.float32) * scale
    )
    return (query_cot, key_cot, value_cot)


def adamw_update(weight, moment_one, moment_two, gradient, rate, decay):
    new_one = beta_one * moment_one + (1.0 - beta_one) * gradient
    new_two = beta_two * moment_two + (1.0 - beta_two) * gradient * gradient
    corrected_one = new_one / (1.0 - beta_one**STEP)
    corrected_two = new_two / (1.0 - beta_two**STEP)
    new_weight = weight - rate * (
        corrected_one / (jnp.sqrt(corrected_two) + adam_eps) + decay * weight
    )
    return (new_weight, new_one, new_two)


def local(
    block_in,
    cotangent,
    routes,
    gate_weights,
    norm_gains,
    attention_weight,
    output_weight,
    w_gate_up,
    w_down,
    m_gains,
    v_gains,
    attention_first_moment,
    attention_second_moment,
    output_first_moment,
    output_second_moment,
    m_gate_up,
    v_gate_up,
    m_down,
    v_down,
):
    bf = jnp.bfloat16
    f32 = jnp.float32
    tok_count = routes.shape[0]
    seq_count = tok_count // SEQ
    width = block_in.shape[1]
    experts = w_gate_up.shape[0]
    rows = w_gate_up.shape[2]
    units = w_gate_up.shape[3]
    cols = attention_weight.shape[2]
    kv_count = cols // HEAD_SIZE
    gains_all = lax.all_gather(norm_gains.astype(bf), "dp", axis=1, tiled=True)
    attn_rows = jnp.concatenate([attention_weight, output_weight], axis=0)
    attn_rows = attn_rows.astype(bf).transpose(1, 0, 2).reshape(rows, 6 * cols)
    attn_all = lax.all_gather(attn_rows, "dp", axis=0, tiled=True)
    proj_all = attn_all[:, : 4 * cols]
    out_all = attn_all[:, 4 * cols :]
    gate_up_rows = w_gate_up.astype(bf).transpose(2, 1, 0, 3).reshape(rows, 2 * experts * units)
    down_rows = w_down.astype(bf).transpose(1, 0, 2).reshape(rows, experts * units)
    cos_table, sine_table = rope_tables(SEQ, HEAD_SIZE)
    gain_one = gains_all[0].astype(f32)
    gain_two = gains_all[1].astype(f32)
    inv_one = lax.rsqrt(jnp.mean(block_in * block_in, axis=1, keepdims=True) + norm_eps)
    normed_one = (block_in * inv_one * gain_one).astype(bf)
    tokens_one = lax.all_gather(normed_one, "tensor", axis=0, tiled=True)
    gate_up_all = lax.all_gather(gate_up_rows, "dp", axis=0, tiled=True)
    down_all = lax.all_gather(down_rows, "dp", axis=0, tiled=True)
    cot_all = lax.all_gather(cotangent.astype(bf), "tensor", axis=0, tiled=True)
    projected = jnp.dot(tokens_one, proj_all, preferred_element_type=f32)
    head_vals = projected.reshape(seq_count, SEQ, 4, kv_count, HEAD_SIZE).transpose(2, 0, 1, 3, 4)
    queries = rotate(head_vals[0:2], cos_table, sine_table).astype(bf).transpose(1, 0, 2, 3, 4)
    keys_rot = rotate(head_vals[2], cos_table, sine_table).astype(bf)
    values = head_vals[3].astype(bf)
    attended, log_totals = lax.map(attend, (queries, keys_rot, values))
    attended_flat = attended.transpose(0, 2, 1, 3, 4).reshape(tok_count, 2 * cols)
    partial_value = jnp.dot(attended_flat, out_all.T, preferred_element_type=f32).astype(bf)
    residual = block_in + lax.psum_scatter(
        partial_value, "tensor", scatter_dimension=0, tiled=True
    ).astype(f32)
    inv_two = lax.rsqrt(jnp.mean(residual * residual, axis=1, keepdims=True) + norm_eps)
    normed_two = (residual * inv_two * gain_two).astype(bf)
    tokens_two = lax.all_gather(normed_two, "tensor", axis=0, tiled=True)
    expert_ids = jnp.arange(experts, dtype=jnp.int32)[None, None, :]
    token_weight = jnp.sum(
        jnp.where(routes[:, :, None] == expert_ids, gate_weights[:, :, None], 0.0), axis=1
    )
    weight_wide = jnp.broadcast_to(token_weight[:, :, None], (tok_count, experts, units)).reshape(
        tok_count, experts * units
    )
    half = experts * units
    gate_up = jnp.dot(tokens_two, gate_up_all, preferred_element_type=f32)
    gate_vals = gate_up[:, :half]
    up_vals = gate_up[:, half:]
    sigmoid_vals = jax.nn.sigmoid(gate_vals)
    hidden = (gate_vals * sigmoid_vals * up_vals * weight_wide).astype(bf)
    hidden_cot = jnp.dot(cot_all, down_all, preferred_element_type=f32) * weight_wide
    gate_cot = (
        hidden_cot * up_vals * sigmoid_vals * (1.0 + gate_vals * (1.0 - sigmoid_vals))
    ).astype(bf)
    up_cot = (hidden_cot * gate_vals * sigmoid_vals).astype(bf)
    both_cot = jnp.concatenate([gate_cot, up_cot], axis=1)
    back_sum = lax.dot_general(
        both_cot, gate_up_all, (((1,), (1,)), ((), ())), preferred_element_type=f32
    ).astype(bf)
    normed_two_cot = lax.psum_scatter(back_sum, "tensor", scatter_dimension=0, tiled=True).astype(
        f32
    )
    down_local = lax.dot_general(
        cot_all, hidden, (((0,), (0,)), ((), ())), preferred_element_type=f32
    ).astype(bf)
    gate_up_local = lax.dot_general(
        tokens_two, both_cot, (((0,), (0,)), ((), ())), preferred_element_type=f32
    ).astype(bf)
    mixture = lax.dot_general(
        hidden, down_all, (((1,), (1,)), ((), ())), preferred_element_type=f32
    ).astype(bf)
    block_out = residual + lax.psum_scatter(
        mixture, "tensor", scatter_dimension=0, tiled=True
    ).astype(f32)
    grad_down = lax.psum_scatter(down_local, "dp", scatter_dimension=0, tiled=True)
    grad_down = grad_down.astype(f32).reshape(rows, experts, units).transpose(1, 0, 2)
    grad_gate_up = lax.psum_scatter(gate_up_local, "dp", scatter_dimension=0, tiled=True)
    grad_gate_up = grad_gate_up.astype(f32).reshape(rows, 2, experts, units).transpose(2, 1, 0, 3)
    scaled_two = gain_two * normed_two_cot
    residual_cot = (
        cotangent
        + inv_two * scaled_two
        - residual * inv_two**3 * jnp.mean(scaled_two * residual, axis=1, keepdims=True)
    )
    resid_all = lax.all_gather(residual_cot.astype(bf), "tensor", axis=0, tiled=True)
    out_local = lax.dot_general(
        resid_all, attended_flat, (((0,), (0,)), ((), ())), preferred_element_type=f32
    )
    attended_cot = jnp.dot(resid_all, out_all, preferred_element_type=f32).astype(bf)
    attended_cot = attended_cot.reshape(seq_count, SEQ, 2, kv_count, HEAD_SIZE).transpose(
        0, 2, 1, 3, 4
    )
    query_cot, key_cot, value_cot = lax.map(
        attend_back, (queries, keys_rot, values, attended, log_totals, attended_cot)
    )
    query_plain = unrotate(query_cot, cos_table, sine_table)
    key_plain = unrotate(key_cot, cos_table, sine_table)
    proj_cot = jnp.concatenate(
        [
            query_plain[:, 0].reshape(tok_count, cols),
            query_plain[:, 1].reshape(tok_count, cols),
            key_plain.reshape(tok_count, cols),
            value_cot.reshape(tok_count, cols),
        ],
        axis=1,
    ).astype(bf)
    attn_local = lax.dot_general(
        tokens_one, proj_cot, (((0,), (0,)), ((), ())), preferred_element_type=f32
    )
    norm_terms = lax.dot_general(
        proj_cot, proj_all, (((1,), (1,)), ((), ())), preferred_element_type=f32
    )
    normed_one_cot = lax.psum_scatter(
        norm_terms.astype(bf), "tensor", scatter_dimension=0, tiled=True
    ).astype(f32)
    both_local = jnp.concatenate([attn_local, out_local], axis=1).astype(bf)
    both_sum = lax.psum_scatter(both_local, "dp", scatter_dimension=0, tiled=True).astype(f32)
    both_sum = both_sum.reshape(rows, 6, cols).transpose(1, 0, 2)
    grad_attn = both_sum[:4]
    grad_out = both_sum[4:]
    scaled_one = gain_one * normed_one_cot
    input_grad = (
        residual_cot
        + inv_one * scaled_one
        - block_in * inv_one**3 * jnp.mean(scaled_one * block_in, axis=1, keepdims=True)
    )
    gain_local = jnp.stack(
        [
            jnp.sum(normed_one_cot * block_in * inv_one, axis=0),
            jnp.sum(normed_two_cot * residual * inv_two, axis=0),
        ]
    )
    gain_sum = lax.psum(gain_local, ("dp", "tensor"))
    grad_gains = lax.dynamic_slice_in_dim(gain_sum, lax.axis_index("dp") * rows, rows, axis=1)
    new_gains, new_m_gains, new_v_gains = adamw_update(
        norm_gains, m_gains, v_gains, grad_gains, rate_gain, 0.0
    )
    new_attn, new_m_attn, new_v_attn = adamw_update(
        attention_weight,
        attention_first_moment,
        attention_second_moment,
        grad_attn,
        rate_matrix,
        decay_matrix,
    )
    new_out, new_m_out, new_v_out = adamw_update(
        output_weight,
        output_first_moment,
        output_second_moment,
        grad_out,
        rate_matrix,
        decay_matrix,
    )
    new_gate_up, new_m_gate_up, new_v_gate_up = adamw_update(
        w_gate_up, m_gate_up, v_gate_up, grad_gate_up, rate_matrix, decay_matrix
    )
    new_down, new_m_down, new_v_down = adamw_update(
        w_down, m_down, v_down, grad_down, rate_matrix, decay_matrix
    )
    return (
        block_out,
        input_grad,
        grad_gains,
        grad_attn,
        grad_out,
        grad_gate_up,
        grad_down,
        new_gains,
        new_attn,
        new_out,
        new_gate_up,
        new_down,
        new_m_gains,
        new_v_gains,
        new_m_attn,
        new_v_attn,
        new_m_out,
        new_v_out,
        new_m_gate_up,
        new_v_gate_up,
        new_m_down,
        new_v_down,
    )


def solution(mesh):
    return jax.shard_map(
        local,
        mesh=mesh,
        in_specs=(
            P(("dp", "tensor"), None),
            P(("dp", "tensor"), None),
            P("dp", None),
            P("dp", None),
            P(None, "dp"),
            P(None, "dp", "tensor"),
            P(None, "dp", "tensor"),
            P(None, None, "dp", "tensor"),
            P(None, "dp", "tensor"),
            P(None, "dp"),
            P(None, "dp"),
            P(None, "dp", "tensor"),
            P(None, "dp", "tensor"),
            P(None, "dp", "tensor"),
            P(None, "dp", "tensor"),
            P(None, None, "dp", "tensor"),
            P(None, None, "dp", "tensor"),
            P(None, "dp", "tensor"),
            P(None, "dp", "tensor"),
        ),
        out_specs=(
            P(("dp", "tensor"), None),
            P(("dp", "tensor"), None),
            P(None, "dp"),
            P(None, "dp", "tensor"),
            P(None, "dp", "tensor"),
            P(None, None, "dp", "tensor"),
            P(None, "dp", "tensor"),
            P(None, "dp"),
            P(None, "dp", "tensor"),
            P(None, "dp", "tensor"),
            P(None, None, "dp", "tensor"),
            P(None, "dp", "tensor"),
            P(None, "dp"),
            P(None, "dp"),
            P(None, "dp", "tensor"),
            P(None, "dp", "tensor"),
            P(None, "dp", "tensor"),
            P(None, "dp", "tensor"),
            P(None, None, "dp", "tensor"),
            P(None, None, "dp", "tensor"),
            P(None, "dp", "tensor"),
            P(None, "dp", "tensor"),
        ),
        check_vma=False,
    )
```

profile of v0, /device:TPU:0, one launch (start us, length us, event | category | flops | bytes accessed | tf_op | source)
XLA Modules:
  0.0 598.8 jit_solution(3122732607899009950)
XLA Ops:
  7.9 10.3 %all_gather.24 = bf16[2,1024]{1,0:T(2,128)(2,1)S(1)} all-gather(bf16[2,128]{1,0:T(2,128)(2,1)S(1)} %convert_element_type.108), channel_id=1, replica_groups=mesh['dp'=8,'tensor'=4] {'dp'}, dimensions={1}, use_global_device_ids=true | all-gather | bytes 4608 | tf_op jit(solution)/shard_map/all_gather | solution.py:143
  25.1 25.1 %all-gather.8.cloned.1.call-done = bf16[512,1024]{1,0:T(8,128)(2,1)} async-done(((bf16[128,1024]{1,0:T(8,128)(2,1)}), bf16[512,1024]{1,0:T(8,128)(2,1)}) %all-gather.8.cloned.1.call-update) | async-done | bytes 1048592 | tf_op jit(solution)/shard_map/all_gather | solution.py:156
  50.2 27.6 %all-gather.10.cloned.1.call-done = bf16[1024,768]{0,1:T(8,128)(2,1)} async-done(((bf16[128,768]{0,1:T(8,128)(2,1)}), bf16[1024,768]{0,1:T(8,128)(2,1)}) %all-gather.10.cloned.1.call-update) | async-done | bytes 1572880 | tf_op jit(solution)/shard_map/all_gather | solution.py:146
  77.8 2.3 fusion.21
  84.6 2.5 convolution_convert_fusion.1
  87.2 27.4 %reduce-scatter.12.cloned.1.call-done = bf16[128,1024]{1,0:T(8,128)(2,1)} async-done(((bf16[512,1024]{1,0:T(8,128)(2,1)}), bf16[128,1024]{1,0:T(8,128)(2,1)}) %reduce-scatter.12.cloned.1.call-update) | async-done | bytes 262160 | tf_op jit(solution)/shard_map/reduce_scatter | solution.py:168
  117.6 2.6 copy.89
  122.1 2.3 copy.91
  127.9 16.3 %all-gather.12.cloned.1.call-done = bf16[512,1024]{1,0:T(8,128)(2,1)} async-done(((bf16[128,1024]{1,0:T(8,128)(2,1)}), bf16[512,1024]{1,0:T(8,128)(2,1)}) %all-gather.12.cloned.1.call-update) | async-done | bytes 1048592 | tf_op jit(solution)/shard_map/all_gather | solution.py:173
  144.2 57.6 %all-gather.14.cloned.1.call-done = bf16[1024,4096]{0,1:T(8,128)(2,1)} async-done(((bf16[128,4096]{0,1:T(8,128)(2,1)}), bf16[1024,4096]{0,1:T(8,128)(2,1)}) %all-gather.14.cloned.1.call-update) | async-done | bytes 8388624 | tf_op jit(solution)/shard_map/all_gather | solution.py:157
  201.8 11.5 %fusion.68 = f32[512,4096]{1,0:T(8,128)} fusion(bf16[512,1024]{1,0:T(8,128)(2,1)} %all-gather.12.cloned.1.call-done, bf16[1024,4096]{0,1:T(8,128)(2,1)} %all-gather.14.cloned.1.call-done), kind=kOutput, calls=%fused_computation.141 | convolution fusion | flops 4294967296 | bytes 17825792 | tf_op jit(solution)/shard_map/dot_general | solution.py:182
  213.3 18.5 %all-gather.18.cloned.1.call-done = bf16[512,1024]{1,0:T(8,128)(2,1)} async-done(((bf16[128,1024]{1,0:T(8,128)(2,1)}), bf16[512,1024]{1,0:T(8,128)(2,1)}) %all-gather.18.cloned.1.call-update) | async-done | bytes 1048592 | tf_op jit(solution)/shard_map/all_gather | solution.py:159
  231.8 39.2 %all-gather.16.cloned.1.call-done = bf16[1024,2048]{0,1:T(8,128)(2,1)} async-done(((bf16[128,2048]{0,1:T(8,128)(2,1)}), bf16[1024,2048]{0,1:T(8,128)(2,1)}) %all-gather.16.cloned.1.call-update) | async-done | bytes 4194320 | tf_op jit(solution)/shard_map/all_gather | solution.py:158
  271.0 2.2 broadcast_in_dim.81
  273.2 10.1 %multiply_convert_fusion.1 = (bf16[512,2048]{1,0:T(8,128)(2,1)S(1)}, bf16[512,2048]{1,0:T(8,128)(2,1)S(1)}, bf16[512,2048]{1,0:T(8,128)(2,1)}) fusion(f32[512,4096]{1,0:T(8,128)} %fusion.68, f32[64,8,16,128]{3,2,1,0:T(8,128)S(1)} %bitcast.152, bf16[512,1024]{1,0:T(8,128)(2,1)} %all-gather.18.cloned.1.call-done, ...), kind=kOutput, calls=%fused_computation.11 | convolution fusion | flops 2166358016 | bytes 24117248 | tf_op jit(solution)/shard_map/dot_general | solution.py:187
  285.4 5.5 fusion.9
  291.1 6.1 %convolution_convert_fusion.4 = bf16[512,1024]{1,0:T(8,128)(2,1)} fusion(bf16[512,2048]{1,0:T(8,128)(2,1)} %get-tuple-element.99, bf16[1024,2048]{0,1:T(8,128)(2,1)} %all-gather.16.cloned.1.call-done), kind=kOutput, calls=%fused_computation.32 | convolution fusion | flops 2148007936 | bytes 7340032 | tf_op jit(solution)/shard_map/dot_general | solution.py:205
  297.3 21.0 %reduce-scatter.16.cloned.1.call-done = bf16[128,1024]{1,0:T(8,128)(2,1)} async-done(((bf16[512,1024]{1,0:T(8,128)(2,1)}), bf16[128,1024]{1,0:T(8,128)(2,1)}) %reduce-scatter.16.cloned.1.call-update) | async-done | bytes 262160 | tf_op jit(solution)/shard_map/reduce_scatter | solution.py:196
  320.5 26.5 %reduce-scatter.14.cloned.1.call-done = bf16[128,1024]{1,0:T(8,128)(2,1)} async-done(((bf16[512,1024]{1,0:T(8,128)(2,1)}), bf16[128,1024]{1,0:T(8,128)(2,1)}) %reduce-scatter.14.cloned.1.call-update) | async-done | bytes 262160 | tf_op jit(solution)/shard_map/reduce_scatter | solution.py:208
  347.0 2.5 fusion.65
  349.6 26.6 %all-gather.20.cloned.1.call-done = bf16[512,1024]{1,0:T(8,128)(2,1)} async-done(((bf16[128,1024]{1,0:T(8,128)(2,1)}), bf16[512,1024]{1,0:T(8,128)(2,1)}) %all-gather.20.cloned.1.call-update) | async-done | bytes 1048592 | tf_op jit(solution)/shard_map/all_gather | solution.py:221
  379.1 3.8 fusion.2
  387.8 2.0 convolution_convert_fusion.2
  391.6 6.1 %convert_bitcast_fusion = bf16[1024,2048]{0,1:T(8,128)(2,1)} fusion(bf16[512,2048]{1,0:T(8,128)(2,1)} %get-tuple-element.99, bf16[512,1024]{1,0:T(8,128)(2,1)S(1)} %copy-done.37), kind=kOutput, calls=%fused_computation.9 | convolution fusion | flops 2149580800 | bytes 7340032 | tf_op jit(solution)/shard_map/dot_general | solution.py:199
  397.7 6.5 %copy.115 = bf16[1024,2048]{1,0:T(8,128)(2,1)} copy(bf16[1024,2048]{0,1:T(8,128)(2,1)} %convert_bitcast_fusion) | data formatting | bytes 8388608
  405.5 9.0 %convolution_convert_fusion = bf16[1024,4096]{1,0:T(8,128)(2,1)} fusion(bf16[512,1024]{1,0:T(8,128)(2,1)S(1)} %copy-done.36, bf16[512,2048]{1,0:T(8,128)(2,1)} %copy-done.40, bf16[512,2048]{1,0:T(8,128)(2,1)} %copy-done.39), kind=kOutput, calls=%fused_computation | convolution fusion | flops 4307550208 | bytes 13631488 | tf_op jit(solution)/shard_map/dot_general | solution.py:202
  416.3 40.0 %psum.7 = f32[2,1024]{1,0:T(2,128)S(1)} all-reduce(f32[2,1024]{1,0:T(2,128)S(1)} %pad_maximum_fusion.14), channel_id=1, replica_groups=mesh['dp'=8,'tensor'=4] {'dp','tensor'}, use_global_device_ids=true, to_apply=%region_13.14 | all-reduce | flops 2048 | bytes 16384 | tf_op jit(solution)/shard_map/psum | solution.py:269
  457.0 1.9 fusion.28
  462.0 47.7 %reduce-scatter.24.cloned.1.call-done = bf16[128,2048]{1,0:T(8,128)(2,1)} async-done(((bf16[1024,2048]{1,0:T(8,128)(2,1)}), bf16[128,2048]{1,0:T(8,128)(2,1)}) %reduce-scatter.24.cloned.1.call-update) | async-done | bytes 524304
  512.3 3.7 multiply_subtract_fusion.1
  516.0 68.6 %reduce-scatter.20.cloned.1.call-done = bf16[128,4096]{1,0:T(8,128)(2,1)} async-done(((bf16[1024,4096]{1,0:T(8,128)(2,1)}), bf16[128,4096]{1,0:T(8,128)(2,1)}) %reduce-scatter.20.cloned.1.call-update) | async-done | bytes 1048592 | tf_op jit(solution)/shard_map/reduce_scatter | solution.py:213
  587.1 4.9 multiply_subtract_fusion
  (173 shorter events, 46.0 us)
Async XLA Ops:
  7.2 43.0 %all-gather.8.cloned.1.call-start = ((), (), s32[]{:S(2)}) async-start(), calls=%async_computation.7 | async-start | bytes 1310720 | tf_op jit(solution)/shard_map/all_gather | solution.py:156
  21.8 56.1 %all-gather.10.cloned.1.call-start = ((), (), s32[]{:S(2)}) async-start(), calls=%async_computation.8 | async-start | bytes 1769472 | tf_op jit(solution)/shard_map/all_gather | solution.py:146
  24.6 89.9 %reduce-scatter.12.cloned.1.call-start = ((), (), s32[]{:S(2)}) async-start(), calls=%async_computation.9 | async-start | bytes 1310720 | tf_op jit(solution)/shard_map/reduce_scatter | solution.py:168
  24.8 58.2 %copy-start.7 = (pred[512,512]{0,1:T(8,128)(4,1)}, pred[512,512]{0,1:T(8,128)(4,1)S(1)}, u32[]{:S(2)}) copy-start(pred[512,512]{0,1:T(8,128)(4,1)S(1)} %iota_compare_fusion) | copy-start | bytes 786436
  84.0 30.5 %copy-start.1 = (f32[128,1024]{1,0:T(8,128)S(1)}, f32[128,1024]{1,0:T(8,128)}, u32[]{:S(2)}) copy-start(f32[128,1024]{1,0:T(8,128)} %param.19) | copy-start | bytes 1572868
  87.1 57.1 %all-gather.12.cloned.1.call-start = ((), (), s32[]{:S(2)}) async-start(), calls=%async_computation.10 | async-start | bytes 1310720 | tf_op jit(solution)/shard_map/all_gather | solution.py:173
  117.6 84.2 %all-gather.14.cloned.1.call-start = ((), (), s32[]{:S(2)}) async-start(), calls=%async_computation.11 | async-start | bytes 9437184 | tf_op jit(solution)/shard_map/all_gather | solution.py:157
  120.2 111.6 %all-gather.18.cloned.1.call-start = ((), (), s32[]{:S(2)}) async-start(), calls=%async_computation.14 | async-start | bytes 1310720 | tf_op jit(solution)/shard_map/all_gather | solution.py:159
  122.0 148.9 %all-gather.16.cloned.1.call-start = ((), (), s32[]{:S(2)}) async-start(), calls=%async_computation.12 | async-start | bytes 4718592 | tf_op jit(solution)/shard_map/all_gather | solution.py:158
  124.4 193.9 %reduce-scatter.16.cloned.1.call-start = ((), (), s32[]{:S(2)}) async-start(), calls=%async_computation.15 | async-start | bytes 1310720 | tf_op jit(solution)/shard_map/reduce_scatter | solution.py:196
  271.0 14.4 %slice-start = ((s8[8388608]{0:T(1024)(128)(4,1)}), s8[4194304]{0:T(1024)(128)(4,1)S(1)}, s32[]{:S(2)}) async-start(s8[8388608]{0:T(1024)(128)(4,1)} %bitcast.179), calls=%async_computation.21 | async-start | bytes 8388608
  273.2 12.1 %slice-start.1 = ((s8[8388608]{0:T(1024)(128)(4,1)}), s8[4194304]{0:T(1024)(128)(4,1)S(1)}, s32[]{:S(2)}) async-start(s8[8388608]{0:T(1024)(128)(4,1)} %bitcast.179), calls=%async_computation.22 | async-start | bytes 8388608
  290.8 56.2 %reduce-scatter.14.cloned.1.call-start = ((), (), s32[]{:S(2)}) async-start(), calls=%async_computation.13 | async-start | bytes 1310720 | tf_op jit(solution)/shard_map/reduce_scatter | solution.py:208
  297.2 78.9 %all-gather.20.cloned.1.call-start = ((), (), s32[]{:S(2)}) async-start(), calls=%async_computation.16 | async-start | bytes 1310720 | tf_op jit(solution)/shard_map/all_gather | solution.py:221
  349.5 29.5 %copy-start.8 = (pred[512,512]{0,1:T(8,128)(4,1)S(1)}, pred[512,512]{0,1:T(8,128)(4,1)}, u32[]{:S(2)}) copy-start(pred[512,512]{0,1:T(8,128)(4,1)} %copy-done.7) | copy-start | bytes 786436
  349.5 65.2 %reduce-scatter.18.cloned.1.call-start = ((), (), s32[]{:S(2)}) async-start(), calls=%async_computation.17 | async-start | bytes 1310720 | tf_op jit(solution)/shard_map/reduce_scatter | solution.py:249
  387.3 71.6 %reduce-scatter.22.cloned.1.call-start = ((), (), s32[]{:S(2)}) async-start(), calls=%async_computation.19 | async-start | bytes 1769472
  391.5 118.2 %reduce-scatter.24.cloned.1.call-start = ((), (), s32[]{:S(2)}) async-start(), calls=%async_computation.20 | async-start | bytes 4718592
  404.3 180.4 %reduce-scatter.20.cloned.1.call-start = ((), (), s32[]{:S(2)}) async-start(), calls=%async_computation.18 | async-start | bytes 9437184 | tf_op jit(solution)/shard_map/reduce_scatter | solution.py:213
  414.5 41.9 %copy-start.32 = (f32[2,128]{1,0:T(2,128)S(1)}, f32[2,128]{1,0:T(2,128)}, u32[]{:S(2)}) copy-start(f32[2,128]{1,0:T(2,128)} %param.23) | copy-start | bytes 3076
  414.5 41.9 %copy-start.33 = (f32[2,128]{1,0:T(2,128)S(1)}, f32[2,128]{1,0:T(2,128)}, u32[]{:S(2)}) copy-start(f32[2,128]{1,0:T(2,128)} %param.28) | copy-start | bytes 3076
  414.5 41.8 %copy-start.34 = (f32[2,128]{1,0:T(2,128)S(1)}, f32[2,128]{1,0:T(2,128)}, u32[]{:S(2)}) copy-start(f32[2,128]{1,0:T(2,128)} %param.29) | copy-start | bytes 3076
  414.5 42.4 %copy-start.10 = (f32[128,1024]{1,0:T(8,128)S(1)}, f32[128,1024]{1,0:T(8,128)}, u32[]{:S(2)}) copy-start(f32[128,1024]{1,0:T(8,128)} %get-tuple-element.94) | copy-start | bytes 1572868
  414.5 42.4 %copy-start.35 = (f32[128]{0:T(128)S(1)}, f32[128]{0:T(128)}, u32[]{:S(2)}) copy-start(f32[128]{0:T(128)} %get-tuple-element.113) | copy-start | bytes 1540
  414.6 45.6 %copy-start.19 = (f32[2,128,128]{2,1,0:T(8,128)S(1)}, f32[2,128,128]{2,1,0:T(8,128)}, u32[]{:S(2)}) copy-start(f32[2,128,128]{2,1,0:T(8,128)} %param.25) | copy-start | bytes 393220
  414.6 45.6 %copy-start.26 = (f32[2,128,128]{2,1,0:T(8,128)S(1)}, f32[2,128,128]{2,1,0:T(8,128)}, u32[]{:S(2)}) copy-start(f32[2,128,128]{2,1,0:T(8,128)} %param.32) | copy-start | bytes 393220
  414.6 45.6 %copy-start.27 = (f32[2,128,128]{2,1,0:T(8,128)S(1)}, f32[2,128,128]{2,1,0:T(8,128)}, u32[]{:S(2)}) copy-start(f32[2,128,128]{2,1,0:T(8,128)} %param.33) | copy-start | bytes 393220
  414.6 46.4 %copy-start.13 = (f32[4,128,128]{2,1,0:T(8,128)S(1)}, f32[4,128,128]{2,1,0:T(8,128)}, u32[]{:S(2)}) copy-start(f32[4,128,128]{2,1,0:T(8,128)} %param.24) | copy-start | bytes 786436
  414.6 46.4 %copy-start.24 = (f32[4,128,128]{2,1,0:T(8,128)S(1)}, f32[4,128,128]{2,1,0:T(8,128)}, u32[]{:S(2)}) copy-start(f32[4,128,128]{2,1,0:T(8,128)} %param.30) | copy-start | bytes 786436
  414.6 46.4 %copy-start.25 = (f32[4,128,128]{2,1,0:T(8,128)S(1)}, f32[4,128,128]{2,1,0:T(8,128)}, u32[]{:S(2)}) copy-start(f32[4,128,128]{2,1,0:T(8,128)} %param.31) | copy-start | bytes 786436
  460.0 52.3 %copy-start.3 = (f32[16,128,128]{2,1,0:T(8,128)S(1)}, f32[16,128,128]{2,1,0:T(8,128)}, u32[]{:S(2)}) copy-start(f32[16,128,128]{2,1,0:T(8,128)} %param.27) | copy-start | bytes 3145732
  516.0 70.5 %copy-start.2 = (f32[16,2,128,128]{3,2,1,0:T(8,128)S(1)}, f32[16,2,128,128]{3,2,1,0:T(8,128)}, u32[]{:S(2)}) copy-start(f32[16,2,128,128]{3,2,1,0:T(8,128)} %param.26) | copy-start | bytes 6291460
  (25 other events, 51.2 us)
Sparse Core Ops, SparseCore 0:
  21.9 28.2 all-gather.7
  52.6 25.1 all-gather.9
  87.3 27.2 reduce-scatter.11
  117.7 26.4 all-gather.11
  146.5 55.2 all-gather.13
  203.8 27.9 all-gather.17
  234.2 36.7 all-gather.15
  291.0 27.2 reduce-scatter.15
  321.2 25.7 reduce-scatter.13
  349.6 26.4 all-gather.19
  387.4 26.6 reduce-scatter.17
  417.8 37.1 reduce-scatter.21
  458.3 51.3 reduce-scatter.23
  513.1 71.4 reduce-scatter.19
where the time goes:
time: 605 us; the launch traced here: 599 us
  waiting for transfers between devices  402 us (66%)
  matrix products  66.3 us (11%)
  blocking collectives  50.3 us (8%)
  other arithmetic  34.6 us (6%)
  local copies, waits for them, and re-layouts  29 us (5%)
  between operations  14.9 us (2%)
    reduce_scatter x1, waiting for transfers between devices, local(): lax.psum_scatter(gate_up_local, 'dp', scatter_dimension=0, tiled=True)  68.6 us
    all_gather x1, waiting for transfers between devices, local(): gate_up_all = lax.all_gather(gate_up_rows, 'dp', axis=0, tiled=True)  57.6 us
    unnamed x16, waiting for transfers between devices  48 us
    psum x1, blocking collectives, local(): gain_sum = lax.psum(gain_local, ('dp', 'tensor'))  40 us
    all_gather x1, waiting for transfers between devices, local(): down_all = lax.all_gather(down_rows, 'dp', axis=0, tiled=True)  39.2 us
    all_gather x1, waiting for transfers between devices, local(): attn_all = lax.all_gather(attn_rows, 'dp', axis=0, tiled=True)  27.6 us
    reduce_scatter x1, waiting for transfers between devices, local(): lax.psum_scatter(partial_value, 'tensor', scatter_dimension=0, tiled=True)  27.4 us
    all_gather x1, waiting for transfers between devices, local(): lax.all_gather(residual_cot.astype(bf), 'tensor', axis=0, tiled=True)  26.6 us
  transfers between devices with their start and end apart: 14, of which 12 were waited for; matrix products, arithmetic and copies ran while one was open for 12% of the time, Pallas kernels for 0%

commit v1 on v0

--- a/solution.py
+++ b/solution.py
@@ -2,6 +2,7 @@
 import jax.numpy as jnp
 from jax import lax
 from jax.sharding import PartitionSpec as P
+from jax.lax import axis_index, ppermute, psum
 
 HEAD_SIZE = 64
 SEQ = 512
@@ -155,7 +156,25 @@
     normed_one = (block_in * inv_one * gain_one).astype(bf)
     tokens_one = lax.all_gather(normed_one, "tensor", axis=0, tiled=True)
     gate_up_all = lax.all_gather(gate_up_rows, "dp", axis=0, tiled=True)
-    down_all = lax.all_gather(down_rows, "dp", axis=0, tiled=True)
+    earlier = psum(1, "dp")
+    wide_out = axis_index("dp")
+    y_new, inter, z2 = (earlier, wide_out, down_rows.shape[0])
+    buffers = tuple((ii * y_new if dev == 0 else ii for dev, ii in enumerate(down_rows.shape)))
+    state_now = jnp.zeros(buffers, down_rows.dtype)
+    down_all = lax.dynamic_update_slice_in_dim(state_now, down_rows, inter * z2, axis=0)
+    piece_next = outer = down_rows
+    for w in range(1, y_new // 2 + 1):
+        moved = tuple(((dev, (dev + 1) % y_new) for dev in range(y_new)))
+        piece_next = ppermute(piece_next, "dp", moved)
+        down_all = lax.dynamic_update_slice_in_dim(
+            down_all, piece_next, (inter - w) % y_new * z2, axis=0
+        )
+        if 2 * w < y_new:
+            mat_out = tuple(((dev, (dev - 1) % y_new) for dev in range(y_new)))
+            outer = ppermute(outer, "dp", mat_out)
+            down_all = lax.dynamic_update_slice_in_dim(
+                down_all, outer, (inter + w) % y_new * z2, axis=0
+            )
     cot_all = lax.all_gather(cotangent.astype(bf), "tensor", axis=0, tiled=True)
     projected = jnp.dot(tokens_one, proj_all, preferred_element_type=f32)
     head_vals = projected.reshape(seq_count, SEQ, 4, kv_count, HEAD_SIZE).transpose(2, 0, 1, 3, 4)

time: 605 us -> 573 us (0.947)
  waiting for transfers between devices: 402 us -> 349 us
  local copies, waits for them, and re-layouts: 29 us -> 41.4 us
  starting transfers between devices: 1.43 us -> 9.48 us
    all_gather x1 -> x0, waiting for transfers between devices: 39.2 us -> none  [local(): down_all = lax.all_gather(down_rows, 'dp', axis=0, tiled=True)]
    ppermute x0 -> x7, waiting for transfers between devices: none -> 32 us  [the longest x3 19.9 us: local(): outer = ppermute(outer, 'dp', mat_out)]
    all_gather x1, waiting for transfers between devices: 57.6 us -> 28 us  [local(): gate_up_all = lax.all_gather(gate_up_rows, 'dp', axis=0, tiled=True)]
    all_gather x1, waiting for transfers between devices: 16.3 us -> 0.01 us  [local(): tokens_two = lax.all_gather(normed_two, 'tensor', axis=0, tiled=True)]
    dynamic_update_slice x0 -> x8, local copies, waits for them, and re-layouts: none -> 11.3 us  [the longest x4 5.68 us: local(): lax.dynamic_update_slice_in_dim(down_all, piece_next, (inter - w) % y_new...]
    ppermute x0 -> x7, starting transfers between devices: none -> 8.56 us  [the longest x3 8.1 us: local(): outer = ppermute(outer, 'dp', mat_out)]
    unnamed x95 -> x103, local copies, waits for them, and re-layouts: 24.7 us -> 23.2 us
    unnamed x16 -> x15, waiting for transfers between devices: 48 us -> 47.8 us
  transfers between devices with their start and end apart: 14 -> 20, of which waited for: 12 -> 14; matrix products, arithmetic and copies ran while one was open for 12% -> 15% of each run, Pallas kernels for 0% -> 0%
where the time goes in v1:
time: 573 us; the launch traced here: 566 us
  waiting for transfers between devices  349 us (61%)
  matrix products  66.5 us (12%)
  blocking collectives  50.3 us (9%)
  local copies, waits for them, and re-layouts  41.4 us (7%)
  other arithmetic  34.5 us (6%)
  between operations  14.9 us (3%)
  starting transfers between devices  9.48 us (2%)
    reduce_scatter x1, waiting for transfers between devices, local(): lax.psum_scatter(gate_up_local, 'dp', scatter_dimension=0, tiled=True)  69.3 us
    unnamed x15, waiting for transfers between devices  47.8 us
    psum x1, blocking collectives, local(): gain_sum = lax.psum(gain_local, ('dp', 'tensor'))  40 us
    all_gather x1, waiting for transfers between devices, local(): gate_up_all = lax.all_gather(gate_up_rows, 'dp', axis=0, tiled=True)  28 us
    all_gather x1, waiting for transfers between devices, local(): attn_all = lax.all_gather(attn_rows, 'dp', axis=0, tiled=True)  27.6 us
    reduce_scatter x1, waiting for transfers between devices, local(): lax.psum_scatter(partial_value, 'tensor', scatter_dimension=0, tiled=True)  27.4 us
    all_gather x1, waiting for transfers between devices, local(): lax.all_gather(residual_cot.astype(bf), 'tensor', axis=0, tiled=True)  26.6 us
    reduce_scatter x1, waiting for transfers between devices, local(): lax.psum_scatter(mixture, 'tensor', scatter_dimension=0, tiled=True)  26.4 us
  transfers between devices with their start and end apart: 20, of which 14 were waited for; matrix products, arithmetic and copies ran while one was open for 15% of the time, Pallas kernels for 0%

profile of v1, /device:TPU:0, one launch (start us, length us, event | category | flops | bytes accessed | tf_op | source)
XLA Modules:
  0.0 566.1 jit_solution(13602315837350771751)
XLA Ops:
  9.7 10.3 %all_gather.21 = bf16[2,1024]{1,0:T(2,128)(2,1)S(1)} all-gather(bf16[2,128]{1,0:T(2,128)(2,1)S(1)} %convert_element_type.108), channel_id=1, replica_groups=mesh['dp'=8,'tensor'=4] {'dp'}, dimensions={1}, use_global_device_ids=true | all-gather | bytes 4608 | tf_op jit(solution)/shard_map/all_gather | solution.py:144
  25.2 25.1 %all-gather.7.cloned.1.call-done = bf16[512,1024]{1,0:T(8,128)(2,1)} async-done(((bf16[128,1024]{1,0:T(8,128)(2,1)}), bf16[512,1024]{1,0:T(8,128)(2,1)}) %all-gather.7.cloned.1.call-update) | async-done | bytes 1048592 | tf_op jit(solution)/shard_map/all_gather | solution.py:157
  50.3 27.6 %all-gather.9.cloned.1.call-done = bf16[1024,768]{0,1:T(8,128)(2,1)} async-done(((bf16[128,768]{0,1:T(8,128)(2,1)}), bf16[1024,768]{0,1:T(8,128)(2,1)}) %all-gather.9.cloned.1.call-update) | async-done | bytes 1572880 | tf_op jit(solution)/shard_map/all_gather | solution.py:147
  83.9 2.5 convolution_convert_fusion.1
  86.5 27.4 %reduce-scatter.12.cloned.1.call-done = bf16[128,1024]{1,0:T(8,128)(2,1)} async-done(((bf16[512,1024]{1,0:T(8,128)(2,1)}), bf16[128,1024]{1,0:T(8,128)(2,1)}) %reduce-scatter.12.cloned.1.call-update) | async-done | bytes 262160 | tf_op jit(solution)/shard_map/reduce_scatter | solution.py:187
  116.9 2.6 copy.92
  121.8 2.6 collective-permute-start.1
  124.4 11.0 %collective-permute-done = bf16[128,2048]{0,1:T(8,128)(2,1)} collective-permute-done((bf16[128,2048]{0,1:T(8,128)(2,1)}, bf16[128,2048]{0,1:T(8,128)(2,1)}, u32[]{:S(2)}, u32[]{:S(2)}) %collective-permute-start) | collective-permute-done | bytes 524320 | tf_op jit(solution)/shard_map/ppermute | solution.py:168
  137.3 2.6 broadcast_in_dim.85
  140.8 2.7 collective-permute-start.3
  149.6 6.3 %collective-permute-done.3 = bf16[128,2048]{0,1:T(8,128)(2,1)} collective-permute-done((bf16[128,2048]{0,1:T(8,128)(2,1)}, bf16[128,2048]{0,1:T(8,128)(2,1)}, u32[]{:S(2)}, u32[]{:S(2)}) %collective-permute-start.3) | collective-permute-done | bytes 524320 | tf_op jit(solution)/shard_map/ppermute | solution.py:174
  155.9 2.8 collective-permute-start.5
  163.9 13.6 %collective-permute-done.5 = bf16[128,2048]{0,1:T(8,128)(2,1)S(1)} collective-permute-done((bf16[128,2048]{0,1:T(8,128)(2,1)}, bf16[128,2048]{0,1:T(8,128)(2,1)S(1)}, u32[]{:S(2)}, u32[]{:S(2)}) %collective-permute-start.5) | collective-permute-done | bytes 524320 | tf_op jit(solution)/shard_map/ppermute | solution.py:174
  180.4 28.0 %all-gather.13.cloned.1.call-done = bf16[1024,4096]{0,1:T(8,128)(2,1)} async-done(((bf16[128,4096]{0,1:T(8,128)(2,1)}), bf16[1024,4096]{0,1:T(8,128)(2,1)}) %all-gather.13.cloned.1.call-update) | async-done | bytes 8388624 | tf_op jit(solution)/shard_map/all_gather | solution.py:158
  208.4 11.6 %fusion.68 = f32[512,4096]{1,0:T(8,128)} fusion(bf16[512,1024]{1,0:T(8,128)(2,1)} %all-gather.11.cloned.1.call-done, bf16[1024,4096]{0,1:T(8,128)(2,1)} %all-gather.13.cloned.1.call-done), kind=kOutput, calls=%fused_computation.149 | convolution fusion | flops 4294967296 | bytes 17825792 | tf_op jit(solution)/shard_map/dot_general | solution.py:201
  220.0 18.4 %all-gather.15.cloned.1.call-done = bf16[512,1024]{1,0:T(8,128)(2,1)} async-done(((bf16[128,1024]{1,0:T(8,128)(2,1)}), bf16[512,1024]{1,0:T(8,128)(2,1)}) %all-gather.15.cloned.1.call-update) | async-done | bytes 1048592 | tf_op jit(solution)/shard_map/all_gather | solution.py:178
  240.7 11.3 %multiply_convert_fusion.1 = (bf16[512,2048]{1,0:T(8,128)(2,1)S(1)}, bf16[512,2048]{1,0:T(8,128)(2,1)S(1)}, bf16[512,2048]{1,0:T(8,128)(2,1)}) fusion(f32[512,4096]{1,0:T(8,128)} %fusion.68, f32[64,8,16,128]{3,2,1,0:T(8,128)S(1)} %bitcast.154, bf16[1024,2048]{0,1:T(8,128)(2,1)} %constant_dynamic-update-slice_fusion, ...), kind=kOutput, calls=%fused_computation.11 | convolution fusion | flops 2166358016 | bytes 24117248 | tf_op jit(solution)/shard_map/dot_general | solution.py:206
  254.0 5.5 fusion.9
  259.7 6.1 %convolution_convert_fusion.4 = bf16[512,1024]{1,0:T(8,128)(2,1)} fusion(bf16[512,2048]{1,0:T(8,128)(2,1)} %get-tuple-element.99, bf16[1024,2048]{0,1:T(8,128)(2,1)} %constant_dynamic-update-slice_fusion), kind=kOutput, calls=%fused_computation.32 | convolution fusion | flops 2148007936 | bytes 7340032 | tf_op jit(solution)/shard_map/dot_general | solution.py:224
  265.9 20.4 %reduce-scatter.16.cloned.1.call-done = bf16[128,1024]{1,0:T(8,128)(2,1)} async-done(((bf16[512,1024]{1,0:T(8,128)(2,1)}), bf16[128,1024]{1,0:T(8,128)(2,1)}) %reduce-scatter.16.cloned.1.call-update) | async-done | bytes 262160 | tf_op jit(solution)/shard_map/reduce_scatter | solution.py:215
  288.6 26.4 %reduce-scatter.14.cloned.1.call-done = bf16[128,1024]{1,0:T(8,128)(2,1)} async-done(((bf16[512,1024]{1,0:T(8,128)(2,1)}), bf16[128,1024]{1,0:T(8,128)(2,1)}) %reduce-scatter.14.cloned.1.call-update) | async-done | bytes 262160 | tf_op jit(solution)/shard_map/reduce_scatter | solution.py:227
  315.0 2.5 fusion.65
  317.6 26.6 %all-gather.17.cloned.1.call-done = bf16[512,1024]{1,0:T(8,128)(2,1)} async-done(((bf16[128,1024]{1,0:T(8,128)(2,1)}), bf16[512,1024]{1,0:T(8,128)(2,1)}) %all-gather.17.cloned.1.call-update) | async-done | bytes 1048592 | tf_op jit(solution)/shard_map/all_gather | solution.py:240
  348.0 2.6 fusion.2
  358.2 6.1 %convert_bitcast_fusion = bf16[1024,2048]{0,1:T(8,128)(2,1)} fusion(bf16[512,2048]{1,0:T(8,128)(2,1)} %get-tuple-element.99, bf16[512,1024]{1,0:T(8,128)(2,1)S(1)} %copy-done.41), kind=kOutput, calls=%fused_computation.9 | convolution fusion | flops 2149580800 | bytes 7340032 | tf_op jit(solution)/shard_map/dot_general | solution.py:218
  364.3 6.5 %copy.120 = bf16[1024,2048]{1,0:T(8,128)(2,1)} copy(bf16[1024,2048]{0,1:T(8,128)(2,1)} %convert_bitcast_fusion) | data formatting | bytes 8388608
  372.1 9.0 %convolution_convert_fusion = bf16[1024,4096]{1,0:T(8,128)(2,1)} fusion(bf16[512,1024]{1,0:T(8,128)(2,1)S(1)} %copy-done.40, bf16[512,2048]{1,0:T(8,128)(2,1)} %copy-done.44, bf16[512,2048]{1,0:T(8,128)(2,1)} %copy-done.43), kind=kOutput, calls=%fused_computation | convolution fusion | flops 4307550208 | bytes 13631488 | tf_op jit(solution)/shard_map/dot_general | solution.py:221
  382.9 40.0 %psum.7 = f32[2,1024]{1,0:T(2,128)S(1)} all-reduce(f32[2,1024]{1,0:T(2,128)S(1)} %pad_maximum_fusion.14), channel_id=1, replica_groups=mesh['dp'=8,'tensor'=4] {'dp','tensor'}, use_global_device_ids=true, to_apply=%region_13.14 | all-reduce | flops 2048 | bytes 16384 | tf_op jit(solution)/shard_map/psum | solution.py:288
  428.7 47.5 %reduce-scatter.24.cloned.1.call-done = bf16[128,2048]{1,0:T(8,128)(2,1)} async-done(((bf16[1024,2048]{1,0:T(8,128)(2,1)}), bf16[128,2048]{1,0:T(8,128)(2,1)}) %reduce-scatter.24.cloned.1.call-update) | async-done | bytes 524304
  477.8 4.2 multiply_subtract_fusion.1
  482.0 69.3 %reduce-scatter.20.cloned.1.call-done = bf16[128,4096]{1,0:T(8,128)(2,1)} async-done(((bf16[1024,4096]{1,0:T(8,128)(2,1)}), bf16[128,4096]{1,0:T(8,128)(2,1)}) %reduce-scatter.20.cloned.1.call-update) | async-done | bytes 1048592 | tf_op jit(solution)/shard_map/reduce_scatter | solution.py:232
  554.4 4.9 multiply_subtract_fusion
  (201 shorter events, 67.1 us)
Async XLA Ops:
  7.2 43.1 %all-gather.7.cloned.1.call-start = ((), (), s32[]{:S(2)}) async-start(), calls=%async_computation.7 | async-start | bytes 1310720 | tf_op jit(solution)/shard_map/all_gather | solution.py:157
  21.8 56.1 %all-gather.9.cloned.1.call-start = ((), (), s32[]{:S(2)}) async-start(), calls=%async_computation.8 | async-start | bytes 1769472 | tf_op jit(solution)/shard_map/all_gather | solution.py:147
  24.7 89.2 %reduce-scatter.12.cloned.1.call-start = ((), (), s32[]{:S(2)}) async-start(), calls=%async_computation.9 | async-start | bytes 1310720 | tf_op jit(solution)/shard_map/reduce_scatter | solution.py:187
  24.9 57.5 %copy-start.8 = (pred[512,512]{0,1:T(8,128)(4,1)}, pred[512,512]{0,1:T(8,128)(4,1)S(1)}, u32[]{:S(2)}) copy-start(pred[512,512]{0,1:T(8,128)(4,1)S(1)} %iota_compare_fusion) | copy-start | bytes 786436
  86.5 94.0 %all-gather.11.cloned.1.call-start = ((), (), s32[]{:S(2)}) async-start(), calls=%async_computation.10 | async-start | bytes 1310720 | tf_op jit(solution)/shard_map/all_gather | solution.py:192
  116.9 91.5 %all-gather.13.cloned.1.call-start = ((), (), s32[]{:S(2)}) async-start(), calls=%async_computation.11 | async-start | bytes 9437184 | tf_op jit(solution)/shard_map/all_gather | solution.py:158
  119.5 118.9 %all-gather.15.cloned.1.call-start = ((), (), s32[]{:S(2)}) async-start(), calls=%async_computation.13 | async-start | bytes 1310720 | tf_op jit(solution)/shard_map/all_gather | solution.py:178
  121.8 13.7 %collective-permute-start = (bf16[128,2048]{0,1:T(8,128)(2,1)}, bf16[128,2048]{0,1:T(8,128)(2,1)}, u32[]{:S(2)}, u32[]{:S(2)}) collective-permute-start(bf16[128,2048]{0,1:T(8,128)(2,1)} %bitcast.159), channel_id=1, source_target_pairs={{0,4},{4,8},{8,12},{12,16},{16,20},{20,24},{24,28},{28,0},{1,5},{5... | collective-permute-start | bytes 1572872 | tf_op jit(solution)/shard_map/ppermute | solution.py:168
  121.8 19.0 %collective-permute-start.1 = (bf16[128,2048]{0,1:T(8,128)(2,1)}, bf16[128,2048]{0,1:T(8,128)(2,1)}, u32[]{:S(2)}, u32[]{:S(2)}) collective-permute-start(bf16[128,2048]{0,1:T(8,128)(2,1)} %bitcast.160), channel_id=1, source_target_pairs={{0,28},{4,0},{8,4},{12,8},{16,12},{20,16},{24,20},{28,24},{1,29},{... | collective-permute-start | bytes 1572872 | tf_op jit(solution)/shard_map/ppermute | solution.py:174
  135.4 10.3 %collective-permute-start.2 = (bf16[128,2048]{0,1:T(8,128)(2,1)}, bf16[128,2048]{0,1:T(8,128)(2,1)}, u32[]{:S(2)}, u32[]{:S(2)}) collective-permute-start(bf16[128,2048]{0,1:T(8,128)(2,1)} %collective-permute-done), channel_id=1, source_target_pairs={{0,4},{4,8},{8,12},{12,16},{16,20},{20,24},{24,28},{28,0},{1,5},{5... | collective-permute-start | bytes 1572872 | tf_op jit(solution)/shard_map/ppermute | solution.py:168
  137.3 149.1 %reduce-scatter.16.cloned.1.call-start = ((), (), s32[]{:S(2)}) async-start(), calls=%async_computation.14 | async-start | bytes 1310720 | tf_op jit(solution)/shard_map/reduce_scatter | solution.py:215
  140.8 15.1 %collective-permute-start.3 = (bf16[128,2048]{0,1:T(8,128)(2,1)}, bf16[128,2048]{0,1:T(8,128)(2,1)}, u32[]{:S(2)}, u32[]{:S(2)}) collective-permute-start(bf16[128,2048]{0,1:T(8,128)(2,1)} %collective-permute-done.1), channel_id=1, source_target_pairs={{0,28},{4,0},{8,4},{12,8},{16,12},{20,16},{24,20},{28,24},{1,29},{... | collective-permute-start | bytes 1572872 | tf_op jit(solution)/shard_map/ppermute | solution.py:174
  145.7 14.9 %collective-permute-start.4 = (bf16[128,2048]{0,1:T(8,128)(2,1)}, bf16[128,2048]{0,1:T(8,128)(2,1)S(1)}, u32[]{:S(2)}, u32[]{:S(2)}) collective-permute-start(bf16[128,2048]{0,1:T(8,128)(2,1)} %collective-permute-done.2), channel_id=1, source_target_pairs={{0,4},{4,8},{8,12},{12,16},{16,20},{20,24},{24,28},{28,0},{1,5},{5... | collective-permute-start | bytes 1572872 | tf_op jit(solution)/shard_map/ppermute | solution.py:168
  155.9 21.6 %collective-permute-start.5 = (bf16[128,2048]{0,1:T(8,128)(2,1)}, bf16[128,2048]{0,1:T(8,128)(2,1)S(1)}, u32[]{:S(2)}, u32[]{:S(2)}) collective-permute-start(bf16[128,2048]{0,1:T(8,128)(2,1)} %collective-permute-done.3), channel_id=1, source_target_pairs={{0,28},{4,0},{8,4},{12,8},{16,12},{20,16},{24,20},{28,24},{1,29},{... | collective-permute-start | bytes 1572872 | tf_op jit(solution)/shard_map/ppermute | solution.py:174
  160.6 18.9 %collective-permute-start.6 = (bf16[128,2048]{0,1:T(8,128)(2,1)S(1)}, bf16[128,2048]{0,1:T(8,128)(2,1)S(1)}, u32[]{:S(2)}, u32[]{:S(2)}) collective-permute-start(bf16[128,2048]{0,1:T(8,128)(2,1)S(1)} %collective-permute-done.4), channel_id=1, source_target_pairs={{0,4},{4,8},{8,12},{12,16},{16,20},{20,24},{24,28},{28,0},{1,5},{5... | collective-permute-start | bytes 1572872 | tf_op jit(solution)/shard_map/ppermute | solution.py:168
  259.5 55.5 %reduce-scatter.14.cloned.1.call-start = ((), (), s32[]{:S(2)}) async-start(), calls=%async_computation.12 | async-start | bytes 1310720 | tf_op jit(solution)/shard_map/reduce_scatter | solution.py:227
  265.9 78.3 %all-gather.17.cloned.1.call-start = ((), (), s32[]{:S(2)}) async-start(), calls=%async_computation.15 | async-start | bytes 1310720 | tf_op jit(solution)/shard_map/all_gather | solution.py:240
  317.5 63.8 %reduce-scatter.18.cloned.1.call-start = ((), (), s32[]{:S(2)}) async-start(), calls=%async_computation.16 | async-start | bytes 1310720 | tf_op jit(solution)/shard_map/reduce_scatter | solution.py:268
  353.8 71.8 %reduce-scatter.22.cloned.1.call-start = ((), (), s32[]{:S(2)}) async-start(), calls=%async_computation.18 | async-start | bytes 1769472
  358.1 118.2 %reduce-scatter.24.cloned.1.call-start = ((), (), s32[]{:S(2)}) async-start(), calls=%async_computation.19 | async-start | bytes 4718592
  370.9 180.4 %reduce-scatter.20.cloned.1.call-start = ((), (), s32[]{:S(2)}) async-start(), calls=%async_computation.17 | async-start | bytes 9437184 | tf_op jit(solution)/shard_map/reduce_scatter | solution.py:232
  381.1 41.9 %copy-start.37 = (f32[2,128]{1,0:T(2,128)S(1)}, f32[2,128]{1,0:T(2,128)}, u32[]{:S(2)}) copy-start(f32[2,128]{1,0:T(2,128)} %param.28) | copy-start | bytes 3076
  381.1 42.5 %copy-start.12 = (f32[128,1024]{1,0:T(8,128)S(1)}, f32[128,1024]{1,0:T(8,128)}, u32[]{:S(2)}) copy-start(f32[128,1024]{1,0:T(8,128)} %get-tuple-element.94) | copy-start | bytes 1572868
  381.1 42.4 %copy-start.39 = (f32[128]{0:T(128)S(1)}, f32[128]{0:T(128)}, u32[]{:S(2)}) copy-start(f32[128]{0:T(128)} %get-tuple-element.113) | copy-start | bytes 1540
  381.2 45.7 %copy-start.21 = (f32[2,128,128]{2,1,0:T(8,128)S(1)}, f32[2,128,128]{2,1,0:T(8,128)}, u32[]{:S(2)}) copy-start(f32[2,128,128]{2,1,0:T(8,128)} %param.25) | copy-start | bytes 393220
  381.2 45.7 %copy-start.28 = (f32[2,128,128]{2,1,0:T(8,128)S(1)}, f32[2,128,128]{2,1,0:T(8,128)}, u32[]{:S(2)}) copy-start(f32[2,128,128]{2,1,0:T(8,128)} %param.32) | copy-start | bytes 393220
  381.2 45.7 %copy-start.29 = (f32[2,128,128]{2,1,0:T(8,128)S(1)}, f32[2,128,128]{2,1,0:T(8,128)}, u32[]{:S(2)}) copy-start(f32[2,128,128]{2,1,0:T(8,128)} %param.33) | copy-start | bytes 393220
  381.2 46.5 %copy-start.15 = (f32[4,128,128]{2,1,0:T(8,128)S(1)}, f32[4,128,128]{2,1,0:T(8,128)}, u32[]{:S(2)}) copy-start(f32[4,128,128]{2,1,0:T(8,128)} %param.24) | copy-start | bytes 786436
  381.2 46.5 %copy-start.26 = (f32[4,128,128]{2,1,0:T(8,128)S(1)}, f32[4,128,128]{2,1,0:T(8,128)}, u32[]{:S(2)}) copy-start(f32[4,128,128]{2,1,0:T(8,128)} %param.30) | copy-start | bytes 786436
  381.2 46.5 %copy-start.27 = (f32[4,128,128]{2,1,0:T(8,128)S(1)}, f32[4,128,128]{2,1,0:T(8,128)}, u32[]{:S(2)}) copy-start(f32[4,128,128]{2,1,0:T(8,128)} %param.31) | copy-start | bytes 786436
  423.6 54.2 %copy-start.4 = (f32[16,128,128]{2,1,0:T(8,128)S(1)}, f32[16,128,128]{2,1,0:T(8,128)}, u32[]{:S(2)}) copy-start(f32[16,128,128]{2,1,0:T(8,128)} %param.27) | copy-start | bytes 3145732
  477.8 75.0 %copy-start.6 = (f32[128,16,128]{2,0,1:T(8,128)}, f32[128,16,128]{2,0,1:T(8,128)S(1)}, u32[]{:S(2)}) copy-start(f32[128,16,128]{2,0,1:T(8,128)S(1)} %copy.102) | copy-start | bytes 3145732
  (35 other events, 256.1 us)
Sparse Core Ops, SparseCore 0:
  21.9 28.2 all-gather.6
  52.7 25.1 all-gather.8
  86.6 27.2 reduce-scatter.11
  117.0 26.4 all-gather.10
  145.8 62.5 all-gather.12
  210.4 27.9 all-gather.14
  259.6 26.6 reduce-scatter.15
  289.2 25.7 reduce-scatter.13
  317.6 26.4 all-gather.16
  354.0 26.6 reduce-scatter.17
  384.5 37.0 reduce-scatter.21
  424.9 51.3 reduce-scatter.23
  479.7 71.4 reduce-scatter.19
